TPU v7x, 256 devices: a whole 4x4x8 slice. The times are simulated.
256 devices in a mesh: section: 8 (over y, x_hi), ctx: 32 (over x_lo, z, core).
Axes of the slice: x: 4 (x_hi: 2, x_lo: 2; x = x_hi * 2 + x_lo), y: 4, z: 8, core: 2. Of those that a mesh axis runs over, the one named last changes fastest.
Arguments:
- latent_state: bfloat16 [8, 5120, 1536], P('section', 'ctx'), may hold values from -20 to 20
- lead_step: int32 [8], replicated, may hold values from 0 to 7, each once
- tail_qkv: bfloat16 [1536, 1280], P(('section', 'ctx')), may hold values from -0.15625 to 0.15625
- tail_out: bfloat16 [1536, 768], P(('section', 'ctx')), may hold values from -0.21875 to 0.21875
- head_qkv: bfloat16 [1536, 1280], P(('section', 'ctx')), may hold values from -0.15625 to 0.15625
- head_out: bfloat16 [1536, 768], P(('section', 'ctx')), may hold values from -0.21875 to 0.21875
- modulation: float32 [2, 2, 9, 1536], replicated, may hold values from 0.5 to 1.5
- qk_gain: float32 [2, 2, 128], replicated, may hold values from 1 to 2
Outputs:
- tail_state: bfloat16 [8, 5120, 1536], P('section', 'ctx')
- head_state: bfloat16 [8, 5120, 1536], P('section', 'ctx')
Inputs may be any that keep to these rules, and one draw needn't show every extreme that they name: `lead_step`: every section holds a different lead time.
All inputs are finite; a program needn't handle non-finite values.
Results may differ from a plain program's by a relative error of at most 0.01.
Values may be sent and summed in bfloat16 or wider, within the bound.
No kernel may reach another device: no remote copies, remote signals or barrier semaphores. Data moves between devices by JAX's collectives and lax.ppermute only.
A program may use at most 64 MiB of HBM per device.

v0:
```python
import jax
import jax.numpy as jnp
from jax import lax
from jax.sharding import PartitionSpec as P

QH = 6
KVH = 2
HD = 128


def passed_along(x, axis, by):
    peers = lax.axis_size(axis)
    return lax.ppermute(x, axis, [(i, (i + by) % peers) for i in range(peers)])


def qk_normal(values, gain_row):
    factor = lax.rsqrt(jnp.mean(values * values, axis=-1, keepdims=True) + 1e-06)
    return (values * factor * gain_row).astype(jnp.bfloat16)


def fetch_weights(joined_w, output_w):
    return (
        lax.all_gather(joined_w, ("section", "ctx"), axis=0, tiled=True),
        lax.all_gather(output_w, ("section", "ctx"), axis=0, tiled=True),
    )


def attend(inputs, joined_w, output_w, gain_rows, q_gain, k_gain):
    tok_rows = inputs.shape[0]
    groups = QH // KVH
    q_width = QH * HD
    k_width = KVH * HD
    score_scale = float(HD) ** (-0.5)
    widened = inputs.astype(jnp.float32)
    factor = lax.rsqrt(jnp.mean(widened * widened, axis=-1, keepdims=True) + 1e-06)
    normed = (widened * factor * gain_rows[0]).astype(jnp.bfloat16)
    projected = jnp.dot(normed, joined_w, preferred_element_type=jnp.float32)
    queries = qk_normal(projected[:, :q_width].reshape(tok_rows, KVH, groups, HD), q_gain)
    key_rows = qk_normal(
        projected[:, q_width : q_width + k_width].reshape(tok_rows, KVH, HD), k_gain
    )
    key_rows = key_rows.reshape(tok_rows, k_width)
    val_rows = projected[:, q_width + k_width :].astype(jnp.bfloat16)

    def add_block(running, key_block, val_block):
        scores = (
            jnp.einsum("tkgd,skd->tkgs", queries, key_block, preferred_element_type=jnp.float32)
            * score_scale
        )
        weights = jnp.exp(scores)
        numerator = running[0] + jnp.einsum(
            "tkgs,skd->tkgd",
            weights.astype(jnp.bfloat16),
            val_block,
            preferred_element_type=jnp.float32,
        )
        return (numerator, running[1] + jnp.sum(weights, axis=-1))

    initial = (
        jnp.zeros((tok_rows, KVH, groups, HD), jnp.float32),
        jnp.zeros((tok_rows, KVH, groups), jnp.float32),
    )
    running = initial
    pieces = (
        lax.all_gather(key_rows, "ctx", axis=0, tiled=True),
        lax.all_gather(val_rows, "ctx", axis=0, tiled=True),
    )
    row_count = pieces[0].shape[0]
    key_piece = pieces[0].reshape(row_count, KVH, HD)
    val_piece = pieces[1].reshape(row_count, KVH, HD)
    key_blocks = key_piece.reshape(row_count // 256, 256, KVH, HD)
    val_blocks = val_piece.reshape(row_count // 256, 256, KVH, HD)

    def step_block(state_pair, block_pair):
        return (add_block(state_pair, block_pair[0], block_pair[1]), None)

    running, unused = lax.scan(step_block, running, (key_blocks, val_blocks))
    numerator, denominator = running
    attended = (numerator / denominator[..., None]).astype(jnp.bfloat16).reshape(tok_rows, q_width)
    update = lax.dot_general(
        attended, output_w, (((1,), (1,)), ((), ())), preferred_element_type=jnp.float32
    )
    return (widened + gain_rows[1] * update).astype(jnp.bfloat16)


def per_device(
    latent_state, lead_step, tail_qkv, tail_out, head_qkv, head_out, modulation, qk_gain
):
    section_pos = lax.axis_index("section")
    section_count = lax.axis_size("section")
    lead_now = lax.dynamic_index_in_dim(lead_step, section_pos, 0, keepdims=False)
    sender = jnp.mod(section_pos - 1 + section_count, section_count)
    lead_next = lax.dynamic_index_in_dim(lead_step, sender, 0, keepdims=False) + 1
    tail_rows = lax.dynamic_index_in_dim(modulation[0], lead_now, 1, keepdims=False)
    head_rows = lax.dynamic_index_in_dim(modulation[1], lead_next, 1, keepdims=False)
    tail_weights = fetch_weights(tail_qkv, tail_out)
    tail_new = attend(
        latent_state[0], tail_weights[0], tail_weights[1], tail_rows, qk_gain[0, 0], qk_gain[0, 1]
    )
    arrived = passed_along(tail_new, "section", 1)
    head_weights = fetch_weights(head_qkv, head_out)
    head_new = attend(
        arrived, head_weights[0], head_weights[1], head_rows, qk_gain[1, 0], qk_gain[1, 1]
    )
    return (tail_new[None], head_new[None])


def solution(mesh):
    in_specs = (
        P("section", "ctx", None),
        P(),
        P(("section", "ctx"), None),
        P(("section", "ctx"), None),
        P(("section", "ctx"), None),
        P(("section", "ctx"), None),
        P(),
        P(),
    )
    out_specs = (P("section", "ctx", None), P("section", "ctx", None))
    return jax.shard_map(
        per_device, mesh=mesh, in_specs=in_specs, out_specs=out_specs, check_vma=False
    )
```

profile of v0, /device:TPU:1, one launch (start us, length us, event | category | flops | bytes accessed | tf_op | source)
XLA Modules:
  0.0 803.6 jit_solution(7002405267562362757)
XLA Ops:
  15.6 115.7 %all-gather.21.cloned.1.call-done = bf16[256,6,1280]{2,1,0:T(8,128)(2,1)} async-done(((bf16[1,6,1280]{2,1,0:T(8,128)(2,1)}), bf16[256,6,1280]{2,1,0:T(8,128)(2,1)}) %all-gather.21.cloned.1.call-update) | async-done | bytes 3932176 | tf_op jit(solution)/shard_map/all_gather | solution.py:23
  131.4 7.3 reshape.102
  138.6 3.0 fusion.19
  144.9 92.6 %all-gather.23.cloned.1.call-done = bf16[256,6,768]{2,1,0:T(8,128)(2,1)} async-done(((bf16[1,6,768]{2,1,0:T(8,128)(2,1)}), bf16[256,6,768]{2,1,0:T(8,128)(2,1)}) %all-gather.23.cloned.1.call-update) | async-done | bytes 2359312 | tf_op jit(solution)/shard_map/all_gather | solution.py:24
  237.5 3.8 reshape.104
  249.6 54.2 %all-gather.15.cloned.1.call-done = bf16[5120,256]{1,0:T(8,128)(2,1)} async-done(((bf16[160,256]{1,0:T(8,128)(2,1)}), bf16[5120,256]{1,0:T(8,128)(2,1)}) %all-gather.15.cloned.1.call-update) | async-done | bytes 2621456 | tf_op jit(solution)/shard_map/all_gather | solution.py:65
  303.8 4.9 reshape_reshape.13
  308.7 62.7 %all-gather.13.cloned.1.call-done = bf16[5120,256]{1,0:T(8,128)(2,1)} async-done(((bf16[160,256]{1,0:T(8,128)(2,1)}), bf16[5120,256]{1,0:T(8,128)(2,1)}) %all-gather.13.cloned.1.call-update) | async-done | bytes 2621456 | tf_op jit(solution)/shard_map/all_gather | solution.py:66
  371.4 4.9 reshape_reshape.12
  376.3 59.0 %while.26 = (s32[]{:T(128)}, f32[160,2,3,128]{3,0,2,1:T(8,128)S(1)}, f32[160,2,3]{0,2,1:T(4,128)S(1)}, bf16[20,256,2,128]{3,2,1,0:T(2,128)(2,1)}, bf16[20,256,2,...) while((s32[]{:T(128)}, f32[160,2,3,128]{3,0,2,1:T(8,128)S(1)}, ...), condition=%wide.region_5.6_spmd.clone, body=%wide.region_3.5_spmd.clone.sunk | while | flops 126813120 | bytes 3013732 | solution.py:77
  435.9 1.9 fusion.11
  437.8 2.5 collective-permute-start
  442.5 47.7 %all-gather.25.cloned.1.call-done = bf16[256,6,1280]{2,1,0:T(8,128)(2,1)} async-done(((bf16[1,6,1280]{2,1,0:T(8,128)(2,1)}), bf16[256,6,1280]{2,1,0:T(8,128)(2,1)}) %all-gather.25.cloned.1.call-update) | async-done | bytes 3932176 | tf_op jit(solution)/shard_map/all_gather | solution.py:23
  490.1 7.2 reshape.106
  497.6 3.0 fusion.21
  502.8 93.4 %all-gather.27.cloned.1.call-done = bf16[256,6,768]{2,1,0:T(8,128)(2,1)} async-done(((bf16[1,6,768]{2,1,0:T(8,128)(2,1)}), bf16[256,6,768]{2,1,0:T(8,128)(2,1)}) %all-gather.27.cloned.1.call-update) | async-done | bytes 2359312 | tf_op jit(solution)/shard_map/all_gather | solution.py:24
  596.2 3.8 reshape.108
  599.9 1.8 slice.75
  608.2 54.2 %all-gather.19.cloned.1.call-done = bf16[5120,256]{1,0:T(8,128)(2,1)} async-done(((bf16[160,256]{1,0:T(8,128)(2,1)}), bf16[5120,256]{1,0:T(8,128)(2,1)}) %all-gather.19.cloned.1.call-update) | async-done | bytes 2621456 | tf_op jit(solution)/shard_map/all_gather | solution.py:65
  662.4 4.9 reshape_reshape.15
  667.3 62.2 %all-gather.17.cloned.1.call-done = bf16[5120,256]{1,0:T(8,128)(2,1)} async-done(((bf16[160,256]{1,0:T(8,128)(2,1)}), bf16[5120,256]{1,0:T(8,128)(2,1)}) %all-gather.17.cloned.1.call-update) | async-done | bytes 2621456 | tf_op jit(solution)/shard_map/all_gather | solution.py:66
  729.6 4.9 reshape_reshape.14
  734.5 58.9 %while.27 = (s32[]{:T(128)}, f32[160,2,3,128]{3,0,2,1:T(8,128)S(1)}, f32[160,2,3]{0,2,1:T(4,128)S(1)}, bf16[20,256,2,128]{3,2,1,0:T(2,128)(2,1)}, bf16[20,256,2,...) while((s32[]{:T(128)}, ...), condition=%wide.region_11.12_spmd.clone, body=%wide.region_9.11_spmd.clone.sunk | while | flops 126813120 | bytes 3013732 | solution.py:77
  794.0 2.7 fusion.12
  (237 shorter events, 145.2 us)
Async XLA Ops:
  7.2 124.2 %all-gather.21.cloned.1.call-start = ((), (), s32[]{:S(2)}) async-start(), calls=%async_computation.4 | async-start | bytes 5263360 | tf_op jit(solution)/shard_map/all_gather | solution.py:23
  7.9 229.6 %all-gather.23.cloned.1.call-start = ((), (), s32[]{:S(2)}) async-start(), calls=%async_computation.5 | async-start | bytes 3158016 | tf_op jit(solution)/shard_map/all_gather | solution.py:24
  8.6 295.2 %all-gather.15.cloned.1.call-start = ((), (), s32[]{:S(2)}) async-start(), calls=%async_computation.1 | async-start | bytes 2703360 | tf_op jit(solution)/shard_map/all_gather | solution.py:65
  15.6 123.0 %copy-start = (bf16[1,160,1536]{2,1,0:T(8,128)(2,1)S(1)}, bf16[1,160,1536]{2,1,0:T(8,128)(2,1)}, u32[]{:S(2)}) copy-start(bf16[1,160,1536]{2,1,0:T(8,128)(2,1)} %param.12) | copy-start | bytes 1474564
  141.6 3.3 copy-start.2
  142.9 228.4 %all-gather.13.cloned.1.call-start = ((), (), s32[]{:S(2)}) async-start(), calls=%async_computation | async-start | bytes 2703360 | tf_op jit(solution)/shard_map/all_gather | solution.py:66
  143.6 346.5 %all-gather.25.cloned.1.call-start = ((), (), s32[]{:S(2)}) async-start(), calls=%async_computation.6 | async-start | bytes 5263360 | tf_op jit(solution)/shard_map/all_gather | solution.py:23
  144.2 451.9 %all-gather.27.cloned.1.call-start = ((), (), s32[]{:S(2)}) async-start(), calls=%async_computation.7 | async-start | bytes 3158016 | tf_op jit(solution)/shard_map/all_gather | solution.py:24
  144.8 517.6 %all-gather.19.cloned.1.call-start = ((), (), s32[]{:S(2)}) async-start(), calls=%async_computation.3 | async-start | bytes 2703360 | tf_op jit(solution)/shard_map/all_gather | solution.py:65
  437.8 59.5 %copy-start.4 = (bf16[160,1536]{1,0:T(8,128)(2,1)}, bf16[160,1536]{1,0:T(8,128)(2,1)S(1)}, u32[]{:S(2)}) copy-start(bf16[160,1536]{1,0:T(8,128)(2,1)S(1)} %fusion.11) | copy-start | bytes 1474564
  437.8 59.5 %collective-permute-start = (bf16[160,1536]{1,0:T(8,128)(2,1)S(1)}, bf16[160,1536]{1,0:T(8,128)(2,1)S(1)}, u32[]{:S(2)}, u32[]{:S(2)}) collective-permute-start(bf16[160,1536]{1,0:T(8,128)(2,1)S(1)} %fusion.11), channel_id=1, source_target_pairs={{0,32},{32,64},{64,96},{96,128},{128,160},{160,192},{192,224},{224... | collective-permute-start | bytes 1474568 | tf_op jit(solution)/shard_map/ppermute | solution.py:13
  497.4 3.2 copy-start.1
  500.6 2.2 copy-start.3
  501.9 227.7 %all-gather.17.cloned.1.call-start = ((), (), s32[]{:S(2)}) async-start(), calls=%async_computation.2 | async-start | bytes 2703360 | tf_op jit(solution)/shard_map/all_gather | solution.py:66
Sparse Core Ops, SparseCore 0:
  11.6 119.7 all-gather.20
  134.9 102.5 all-gather.22
  239.4 64.3 all-gather.14
  306.1 65.2 all-gather.12
  374.8 115.3 all-gather.24
  493.5 102.5 all-gather.26
  598.0 64.3 all-gather.18
  664.3 65.2 all-gather.16
where the time goes:
time: 807 us; the launch traced here: 804 us
  waiting for transfers between devices  585 us (72%)
  local copies, waits for them, and re-layouts  106 us (13%)
  matrix products  80.5 us (10%)
  between operations  17.7 us (2%)
  other arithmetic  9.34 us (1%)
    all_gather x2, waiting for transfers between devices, fetch_weights(): lax.all_gather(output_w, ('section', 'ctx'), axis=0, tiled=True)  186 us
    all_gather x2, waiting for transfers between devices, fetch_weights(): lax.all_gather(joined_w, ('section', 'ctx'), axis=0, tiled=True)  163 us
    all_gather x2, waiting for transfers between devices, attend(): lax.all_gather(val_rows, 'ctx', axis=0, tiled=True)  125 us
    all_gather x2, waiting for transfers between devices, attend(): lax.all_gather(key_rows, 'ctx', axis=0, tiled=True)  108 us
    dot_general x40, matrix products, add_block(): jnp.einsum('tkgd,skd->tkgs', queries, key_block, preferred_element_type=j...  56.5 us
    dynamic_slice x40, local copies, waits for them, and re-layouts, attend(): running, unused = lax.scan(step_block, running, (key_blocks, val_blocks))  46.1 us
    unnamed x16, local copies, waits for them, and re-layouts  23.5 us
  transfers between devices with their start and end apart: 9, of which 8 were waited for; matrix products, arithmetic and copies ran while one was open for 16% of the time, Pallas kernels for 0%

commit v1 on v0

--- a/solution.py
+++ b/solution.py
@@ -19,10 +19,13 @@
 
 
 def fetch_weights(joined_w, output_w):
-    return (
-        lax.all_gather(joined_w, ("section", "ctx"), axis=0, tiled=True),
-        lax.all_gather(output_w, ("section", "ctx"), axis=0, tiled=True),
-    )
+
+    def begin_spot(message):
+        last = jnp.stack([message for _ in range(lax.axis_size(("section", "ctx")))], axis=0)
+        tile_out = lax.all_to_all(last, axis_name=("section", "ctx"), split_axis=0, concat_axis=0)
+        return jnp.concatenate(tile_out, axis=0)
+
+    return (lax.all_gather(joined_w, ("section", "ctx"), axis=0, tiled=True), begin_spot(output_w))
 
 
 def attend(inputs, joined_w, output_w, gain_rows, q_gain, k_gain):

time: 807 us -> 638 us (0.79)
  waiting for transfers between devices: 585 us -> 393 us
  starting transfers between devices: 2.99 us -> 22.4 us
    all_gather x2 -> x0, waiting for transfers between devices: 186 us -> none  [fetch_weights(): lax.all_gather(output_w, ('section', 'ctx'), axis=0, tiled=True)]
    all_to_all x0 -> x2, waiting for transfers between devices: none -> 177 us  [begin_spot(): lax.all_to_all(last, axis_name=('section', 'ctx'), split_axis=0, concat_a...]
    all_gather x2, waiting for transfers between devices: 108 us -> 0.01 us  [attend(): lax.all_gather(key_rows, 'ctx', axis=0, tiled=True)]
    all_gather x2, waiting for transfers between devices: 125 us -> 50.1 us  [attend(): lax.all_gather(val_rows, 'ctx', axis=0, tiled=True)]
    all_to_all x0 -> x2, starting transfers between devices: none -> 19.2 us  [begin_spot(): lax.all_to_all(last, axis_name=('section', 'ctx'), split_axis=0, concat_a...]
    unnamed x16 -> x18, local copies, waits for them, and re-layouts: 23.5 us -> 16.1 us
  transfers between devices with their start and end apart: 9 -> 9, of which waited for: 8 -> 6; matrix products, arithmetic and copies ran while one was open for 16% -> 19% of each run, Pallas kernels for 0% -> 0%
where the time goes in v1:
time: 638 us; the launch traced here: 634 us
  waiting for transfers between devices  393 us (62%)
  local copies, waits for them, and re-layouts  110 us (17%)
  matrix products  80.5 us (13%)
  starting transfers between devices  22.4 us (4%)
  between operations  17.8 us (3%)
  other arithmetic  9.32 us (1%)
    all_to_all x2, waiting for transfers between devices, begin_spot(): lax.all_to_all(last, axis_name=('section', 'ctx'), split_axis=0, concat_a...  177 us
    all_gather x2, waiting for transfers between devices, fetch_weights(): lax.all_gather(joined_w, ('section', 'ctx'), axis=0, tiled=True)  164 us
    dot_general x40, matrix products, add_block(): jnp.einsum('tkgd,skd->tkgs', queries, key_block, preferred_element_type=j...  56.5 us
    all_gather x2, waiting for transfers between devices, attend(): lax.all_gather(val_rows, 'ctx', axis=0, tiled=True)  50.1 us
    dynamic_slice x40, local copies, waits for them, and re-layouts, attend(): running, unused = lax.scan(step_block, running, (key_blocks, val_blocks))  46.1 us
    all_to_all x2, starting transfers between devices, begin_spot(): lax.all_to_all(last, axis_name=('section', 'ctx'), split_axis=0, concat_a...  19.2 us
    unnamed x18, local copies, waits for them, and re-layouts  16.1 us
    dot_general x40, matrix products, add_block(): jnp.einsum('tkgs,skd->tkgd', weights.astype(jnp.bfloat16), val_block, pre...  13.3 us
  transfers between devices with their start and end apart: 9, of which 6 were waited for; matrix products, arithmetic and copies ran while one was open for 19% of the time, Pallas kernels for 0%

profile of v1, /device:TPU:1, one launch (start us, length us, event | category | flops | bytes accessed | tf_op | source)
XLA Modules:
  0.0 634.4 jit_solution(18444111928200730918)
XLA Ops:
  14.9 116.4 %all-gather.17.cloned.1.call-done = bf16[256,6,1280]{2,1,0:T(8,128)(2,1)} async-done(((bf16[1,6,1280]{2,1,0:T(8,128)(2,1)}), bf16[256,6,1280]{2,1,0:T(8,128)(2,1)}) %all-gather.17.cloned.1.call-update) | async-done | bytes 3932176 | tf_op jit(solution)/shard_map/all_gather | solution.py:28
  131.4 7.3 %reshape.114 = bf16[1536,1280]{1,0:T(8,128)(2,1)} reshape(bf16[256,6,1280]{2,1,0:T(8,128)(2,1)} %all-gather.17.cloned.1.call-done) | data formatting | bytes 7864320
  138.6 3.0 fusion.19
  143.7 1.9 stack.4
  145.6 9.6 %all-to-all-start = ((bf16[256,6,768]{2,1,0:T(8,128)(2,1)}), bf16[256,6,768]{2,1,0:T(8,128)(2,1)}, u32[]{:S(2)}, u32[]{:S(2)}) async-start(bf16[256,6,768]{2,1,0:T(8,128)(2,1)} %stack.4), calls=%async_computation | async-start | bytes 6291456 | tf_op jit(solution)/shard_map/all_to_all | solution.py:25
  155.8 88.1 %all-to-all-done = bf16[256,6,768]{2,1,0:T(8,128)(2,1)} async-done(((bf16[256,6,768]{2,1,0:T(8,128)(2,1)}), bf16[256,6,768]{2,1,0:T(8,128)(2,1)}, u32[]{:S(2)}, u32[]{:S(2)}) %all-to-all-start) | async-done | bytes 2359328 | tf_op jit(solution)/shard_map/all_to_all | solution.py:25
  244.0 3.8 reshape.108
  256.0 4.9 reshape_reshape.13
  260.9 25.8 %all-gather.9.cloned.1.call-done = bf16[5120,256]{1,0:T(8,128)(2,1)} async-done(((bf16[160,256]{1,0:T(8,128)(2,1)}), bf16[5120,256]{1,0:T(8,128)(2,1)}) %all-gather.9.cloned.1.call-update) | async-done | bytes 2621456 | tf_op jit(solution)/shard_map/all_gather | solution.py:69
  286.8 4.9 reshape_reshape.12
  291.7 59.0 %while.26 = (s32[]{:T(128)}, f32[160,2,3,128]{3,0,2,1:T(8,128)S(1)}, f32[160,2,3]{0,2,1:T(4,128)S(1)}, bf16[20,256,2,128]{3,2,1,0:T(2,128)(2,1)}, bf16[20,256,2,...) while((s32[]{:T(128)}, f32[160,2,3,128]{3,0,2,1:T(8,128)S(1)}, ...), condition=%wide.region_5.6_spmd.clone, body=%wide.region_3.5_spmd.clone.sunk | while | flops 126813120 | bytes 3013732 | solution.py:80
  351.2 1.9 fusion.11
  353.2 2.9 collective-permute-start
  358.3 47.5 %all-gather.19.cloned.1.call-done = bf16[256,6,1280]{2,1,0:T(8,128)(2,1)} async-done(((bf16[1,6,1280]{2,1,0:T(8,128)(2,1)}), bf16[256,6,1280]{2,1,0:T(8,128)(2,1)}) %all-gather.19.cloned.1.call-update) | async-done | bytes 3932176 | tf_op jit(solution)/shard_map/all_gather | solution.py:28
  405.8 7.3 %reshape.116 = bf16[1536,1280]{1,0:T(8,128)(2,1)} reshape(bf16[256,6,1280]{2,1,0:T(8,128)(2,1)} %all-gather.19.cloned.1.call-done) | data formatting | bytes 7864320
  413.3 3.0 fusion.21
  419.5 9.6 %all-to-all-start.1 = ((bf16[256,6,768]{2,1,0:T(8,128)(2,1)}), bf16[256,6,768]{2,1,0:T(8,128)(2,1)}, u32[]{:S(2)}, u32[]{:S(2)}) async-start(bf16[256,6,768]{2,1,0:T(8,128)(2,1)} %stack.5), calls=%async_computation.1 | async-start | bytes 6291456 | tf_op jit(solution)/shard_map/all_to_all | solution.py:25
  430.0 89.1 %all-to-all-done.1 = bf16[256,6,768]{2,1,0:T(8,128)(2,1)} async-done(((bf16[256,6,768]{2,1,0:T(8,128)(2,1)}), bf16[256,6,768]{2,1,0:T(8,128)(2,1)}, u32[]{:S(2)}, u32[]{:S(2)}) %all-to-all-start.1) | async-done | bytes 2359328 | tf_op jit(solution)/shard_map/all_to_all | solution.py:25
  519.1 3.8 reshape.111
  531.2 4.9 reshape_reshape.15
  536.1 24.3 %all-gather.13.cloned.1.call-done = bf16[5120,256]{1,0:T(8,128)(2,1)} async-done(((bf16[160,256]{1,0:T(8,128)(2,1)}), bf16[5120,256]{1,0:T(8,128)(2,1)}) %all-gather.13.cloned.1.call-update) | async-done | bytes 2621456 | tf_op jit(solution)/shard_map/all_gather | solution.py:69
  560.4 4.9 reshape_reshape.14
  565.3 58.9 %while.27 = (s32[]{:T(128)}, f32[160,2,3,128]{3,0,2,1:T(8,128)S(1)}, f32[160,2,3]{0,2,1:T(4,128)S(1)}, bf16[20,256,2,128]{3,2,1,0:T(2,128)(2,1)}, bf16[20,256,2,...) while((s32[]{:T(128)}, ...), condition=%wide.region_11.12_spmd.clone, body=%wide.region_9.11_spmd.clone.sunk | while | flops 126813120 | bytes 3013732 | solution.py:80
  624.8 2.7 fusion.12
  (241 shorter events, 147.6 us)
Async XLA Ops:
  7.2 124.2 %all-gather.17.cloned.1.call-start = ((), (), s32[]{:S(2)}) async-start(), calls=%async_computation.6 | async-start | bytes 5263360 | tf_op jit(solution)/shard_map/all_gather | solution.py:28
  7.9 248.1 %all-gather.11.cloned.1.call-start = ((), (), s32[]{:S(2)}) async-start(), calls=%async_computation.3 | async-start | bytes 2703360 | tf_op jit(solution)/shard_map/all_gather | solution.py:68
  14.9 123.7 %copy-start = (bf16[1,160,1536]{2,1,0:T(8,128)(2,1)S(1)}, bf16[1,160,1536]{2,1,0:T(8,128)(2,1)}, u32[]{:S(2)}) copy-start(bf16[1,160,1536]{2,1,0:T(8,128)(2,1)} %param.12) | copy-start | bytes 1474564
  138.6 5.0 copy-start.5
  141.6 4.0 copy-start.2
  142.9 143.8 %all-gather.9.cloned.1.call-start = ((), (), s32[]{:S(2)}) async-start(), calls=%async_computation.2 | async-start | bytes 2703360 | tf_op jit(solution)/shard_map/all_gather | solution.py:69
  145.6 98.4 %all-to-all-start = ((bf16[256,6,768]{2,1,0:T(8,128)(2,1)}), bf16[256,6,768]{2,1,0:T(8,128)(2,1)}, u32[]{:S(2)}, u32[]{:S(2)}) async-start(bf16[256,6,768]{2,1,0:T(8,128)(2,1)} %stack.4), calls=%async_computation | async-start | bytes 6291456 | tf_op jit(solution)/shard_map/all_to_all | solution.py:25
  155.2 250.6 %all-gather.19.cloned.1.call-start = ((), (), s32[]{:S(2)}) async-start(), calls=%async_computation.7 | async-start | bytes 5263360 | tf_op jit(solution)/shard_map/all_gather | solution.py:28
  155.8 375.4 %all-gather.15.cloned.1.call-start = ((), (), s32[]{:S(2)}) async-start(), calls=%async_computation.5 | async-start | bytes 2703360 | tf_op jit(solution)/shard_map/all_gather | solution.py:68
  353.2 59.9 %copy-start.4 = (bf16[160,1536]{1,0:T(8,128)(2,1)}, bf16[160,1536]{1,0:T(8,128)(2,1)S(1)}, u32[]{:S(2)}) copy-start(bf16[160,1536]{1,0:T(8,128)(2,1)S(1)} %fusion.11) | copy-start | bytes 1474564
  353.2 59.9 %collective-permute-start = (bf16[160,1536]{1,0:T(8,128)(2,1)S(1)}, bf16[160,1536]{1,0:T(8,128)(2,1)S(1)}, u32[]{:S(2)}, u32[]{:S(2)}) collective-permute-start(bf16[160,1536]{1,0:T(8,128)(2,1)S(1)} %fusion.11), channel_id=1, source_target_pairs={{0,32},{32,64},{64,96},{96,128},{128,160},{160,192},{192,224},{224... | collective-permute-start | bytes 1474568 | tf_op jit(solution)/shard_map/ppermute | solution.py:13
  413.1 3.2 copy-start.1
  413.3 4.3 copy-start.6
  416.3 13.0 %copy-start.3 = (f32[160,1280]{1,0:T(8,128)}, f32[160,1280]{1,0:T(8,128)S(1)}, u32[]{:S(2)}) copy-start(f32[160,1280]{1,0:T(8,128)S(1)} %fusion.21) | copy-start | bytes 2457604
  419.5 99.6 %all-to-all-start.1 = ((bf16[256,6,768]{2,1,0:T(8,128)(2,1)}), bf16[256,6,768]{2,1,0:T(8,128)(2,1)}, u32[]{:S(2)}, u32[]{:S(2)}) async-start(bf16[256,6,768]{2,1,0:T(8,128)(2,1)} %stack.5), calls=%async_computation.1 | async-start | bytes 6291456 | tf_op jit(solution)/shard_map/all_to_all | solution.py:25
  429.1 131.3 %all-gather.13.cloned.1.call-start = ((), (), s32[]{:S(2)}) async-start(), calls=%async_computation.4 | async-start | bytes 2703360 | tf_op jit(solution)/shard_map/all_gather | solution.py:69
Sparse Core Ops, SparseCore 0:
  11.6 119.7 all-gather.16
  143.1 74.0 all-gather.10
  219.6 67.1 all-gather.8
  290.2 115.5 all-gather.18
  417.7 73.6 all-gather.14
  493.1 67.2 all-gather.12
